TPU v7x, 256 devices: a whole 4x4x8 slice. The times are simulated.
256 devices in a mesh: seq: 32 (over z, y), exp: 8 (over x, core).
Axes of the slice: x: 4, y: 4, z: 8, core: 2. Of those that a mesh axis runs over, the one named last changes fastest.
Arguments:
- residual: bfloat16 [4096, 6144], P('exp', 'seq'), may hold values from -8 to 8
- query: bfloat16 [4096, 8192], P('seq', 'exp'), may hold values from -6 to 6
- key_in: bfloat16 [4096, 8192], P('seq', 'exp'), may hold values from -6 to 6
- value_in: bfloat16 [4096, 8192], P('seq', 'exp'), may hold values from -0.75 to 0.75
- gate_in: bfloat16 [4096, 8192], P('seq', 'exp'), may hold values from -6 to 6
- log_decay: float32 [4096, 64], P('seq', 'exp'), may hold values from -2 to 0
- state_in: float32 [64, 128, 128], P('exp'), may hold values from -12 to 12
- attn_gain: float32 [8192], P('exp'), may hold values from 0.1 to 1.9
- w_out: bfloat16 [8192, 6144], P('exp', 'seq'), may hold values from -0.0625 to 0.0625
- moe_gain: float32 [6144], P('seq'), may hold values from 0.1 to 1.9
- router: float32 [6144, 32], P('seq'), may hold values from -0.078125 to 0.078125
- w_gate: bfloat16 [8, 9216, 6144], P('exp', 'seq'), may hold values from -0.078125 to 0.078125
- w_up: bfloat16 [8, 9216, 6144], P('exp', 'seq'), may hold values from -0.078125 to 0.078125
- w_down: bfloat16 [8, 9216, 6144], P('exp', None, 'seq'), may hold values from -0.125 to 0.125
- expert_ids: int32 [4096, 2], P('exp'), may hold values from 0 to 31, all different within a row; in each aligned block of 512 rows (0 to 511, 512 to 1023, ...) at most 40 rows name the same one
- keep_counts: int32 [32], replicated, may hold values from 64 to 319
Outputs:
- layer_out: bfloat16 [4096, 6144], P('exp', 'seq')
- final_state: float32 [64, 128, 128], P('exp', 'seq')
Inputs may be any that keep to these rules, and one draw needn't show every extreme that they name: `expert_ids`: each row names 2 different experts. Among the rows of one device no expert is named more than 40 times, a bound that some block reaches.
All inputs are finite; a program needn't handle non-finite values.
Results may differ from a plain program's by a relative error of at most 0.014.
Values may be sent and summed in bfloat16 or wider, within the bound.
A program may use at most 128 MiB of HBM per device.

v0:
```python
import jax
import jax.numpy as jnp
from jax import lax
from jax.sharding import PartitionSpec as P

D = 6144
epsilon = 1e-05
highest = lax.Precision.HIGHEST


def entering(x, axis, join, neutral):
    place = lax.axis_index(axis)
    gathered = jax.tree.map(
        lambda a, kind: lax.all_gather(a.astype(kind), axis), x, (jnp.bfloat16, jnp.bfloat16)
    )
    state = jax.tree.map(lambda a, e: jnp.zeros_like(a) + jnp.asarray(e, a.dtype), x, neutral)

    def one(lap, state):
        return join(
            state,
            jax.tree.map(
                lambda a, own: lax.dynamic_index_in_dim(a, lap, 0, False).astype(own.dtype),
                gathered,
                x,
            ),
        )

    return lax.fori_loop(0, place, one, state)


def broadcast(value, axis, source):
    kept = jnp.where(lax.axis_index(axis) == source, value, 0).astype(value.dtype)
    return lax.psum(kept, axis)


def entering_2(part, axis, combine, identity):
    place = lax.axis_index(axis)
    gathered = lax.all_gather(part, axis)
    state = jnp.zeros_like(part) + jnp.asarray(identity, part.dtype)

    def one(lap, state):
        return combine(state, lax.dynamic_index_in_dim(gathered, lap, 0, False))

    return lax.fori_loop(0, place, one, state)


def block_terms(act_query, act_key, val_rows, log_rows):
    running_log = jnp.cumsum(log_rows, axis=0)
    block_log = running_log[-1]
    length = log_rows.shape[0]
    causal_mask = (jnp.arange(length)[:, None] >= jnp.arange(length)[None, :])[None]
    flipped = jnp.transpose(running_log)
    log_gap = flipped[:, :, None] - flipped[:, None, :]
    decay_rows = jnp.where(causal_mask, jnp.exp(jnp.where(causal_mask, log_gap, 0.0)), 0.0)
    scores = jnp.einsum("thd,shd->hts", act_query, act_key, precision=highest)
    local_part = jnp.einsum("hts,shd->thd", scores * decay_rows, val_rows, precision=highest)
    tail_decay = jnp.exp(block_log[None, :] - running_log)
    update = jnp.einsum(
        "shd,she->hde", act_key * tail_decay[:, :, None], val_rows, precision=highest
    )
    return (local_part, running_log, block_log, update)


def from_state(act_query, running_log, state_carry):
    return jnp.einsum(
        "thd,hde->the", act_query * jnp.exp(running_log)[:, :, None], state_carry, precision=highest
    )


def join_states(earlier, later_part):
    return (
        earlier[0] + later_part[0],
        jnp.exp(later_part[0])[:, None, None] * earlier[1] + later_part[1],
    )


def add_counts(earlier, later_counts):
    return earlier + later_counts


def local(
    residual,
    query,
    key_in,
    value_in,
    gate_in,
    log_decay,
    state_in,
    attn_gain,
    w_out,
    moe_gain,
    router,
    w_gate,
    w_up,
    w_down,
    expert_ids,
    keep_counts,
):
    tok_rows, head_width = query.shape
    head_count = log_decay.shape[1]
    head_size = head_width // head_count
    act_query = jax.nn.silu(query.astype(jnp.float32)).reshape(tok_rows, head_count, head_size)
    act_key = jax.nn.silu(key_in.astype(jnp.float32)).reshape(tok_rows, head_count, head_size)
    val_rows = value_in.astype(jnp.float32).reshape(tok_rows, head_count, head_size)
    local_part, running_log, block_log, update = block_terms(
        act_query, act_key, val_rows, log_decay
    )
    segments = lax.axis_size("seq")
    position = lax.axis_index("seq")
    row_share = head_size // segments
    identity_pair = (jnp.zeros_like(block_log), jnp.zeros_like(update))
    before_log, before_state = entering((block_log, update), "seq", join_states, identity_pair)
    incoming = jnp.exp(before_log)[:, None, None] * state_in + before_state
    through = jnp.exp(block_log)[:, None, None] * incoming + update
    last_whole = broadcast(through.astype(jnp.bfloat16), "seq", segments - 1).astype(through.dtype)
    final_rows = lax.dynamic_slice_in_dim(last_whole, position * row_share, row_share, 1)
    outputs = local_part + from_state(act_query, running_log, incoming)
    square_mean = jnp.mean(outputs * outputs, axis=2, keepdims=True)
    normed = outputs * lax.rsqrt(square_mean + epsilon) * attn_gain.reshape(head_count, head_size)
    heads_mixed = (
        normed.reshape(tok_rows, head_width) * jax.nn.sigmoid(gate_in.astype(jnp.float32))
    ).astype(jnp.bfloat16)
    gathered = lax.all_gather(heads_mixed, "seq", axis=0, tiled=True)
    block_rows = residual.shape[0]
    projected = lax.psum_scatter(
        jnp.dot(gathered, w_out, preferred_element_type=jnp.float32).astype(jnp.bfloat16),
        "exp",
        scatter_dimension=0,
        tiled=True,
    ).astype(jnp.float32)
    after_attn = residual.astype(jnp.float32) + projected
    experts_all = router.shape[1]
    logit_part = jnp.dot(after_attn * moe_gain, router, precision=highest)
    choose = (
        expert_ids[:, :, None] == jnp.arange(experts_all, dtype=jnp.int32)[None, None, :]
    ).astype(jnp.float32)
    chosen_part = jnp.einsum("tke,te->tk", choose, logit_part, precision=highest)
    squares, chosen = lax.psum((jnp.sum(after_attn * after_attn, axis=1), chosen_part), "seq")
    inv_rms = lax.rsqrt(squares / D + epsilon)
    chosen = chosen * inv_rms[:, None]
    gate_probs = jnp.stack(
        [jax.nn.sigmoid(chosen[:, 0] - chosen[:, 1]), jax.nn.sigmoid(chosen[:, 1] - chosen[:, 0])],
        axis=1,
    )
    routed_in = (after_attn * inv_rms[:, None] * moe_gain).astype(jnp.bfloat16)
    lanes = lax.axis_size("exp")
    window = w_gate.shape[0] * lanes
    capacity = 5 * block_rows * lanes // (2 * lanes * experts_all)
    top_count = expert_ids.shape[1]
    flat_ids = expert_ids.reshape(block_rows * top_count)
    onehot = (flat_ids[:, None] == jnp.arange(window, dtype=jnp.int32)[None, :]).astype(jnp.int32)
    local_rank = jnp.sum((jnp.cumsum(onehot, axis=0) - onehot) * onehot, axis=1)
    before = entering_2(jnp.sum(onehot, axis=0), "exp", add_counts, jnp.zeros((window,), jnp.int32))
    global_rank = local_rank + jnp.sum(before[None, :] * onehot, axis=1)
    limits = jnp.sum(keep_counts[None, :window] * onehot, axis=1)
    is_kept = (flat_ids < window) & (global_rank < limits)
    slot_hot = ((local_rank[:, None] == jnp.arange(capacity)[None, :]) & is_kept[:, None]).astype(
        jnp.int32
    )
    assign_int = onehot[:, :, None] * slot_hot[:, None, :]
    assign_table = assign_int.astype(jnp.bfloat16)
    token_table = jnp.sum(
        assign_int.reshape(block_rows, top_count, window, capacity), axis=1
    ).astype(jnp.bfloat16)
    sending = jnp.einsum(
        "tec,td->ecd", token_table, routed_in, preferred_element_type=jnp.float32
    ).astype(jnp.bfloat16)
    arrived = lax.all_to_all(sending, "exp", split_axis=0, concat_axis=1, tiled=True)
    contract_dims = (((1,), (1,)), ((), ()))
    portion = lax.all_gather(arrived, "seq", axis=2, tiled=True)
    gate_cols = w_gate[0]
    up_cols = w_up[0]
    gate_add = lax.dot_general(
        portion[0], gate_cols, contract_dims, preferred_element_type=jnp.float32
    )
    up_add = lax.dot_general(portion[0], up_cols, contract_dims, preferred_element_type=jnp.float32)
    hidden = (jax.nn.silu(gate_add) * up_add).astype(jnp.bfloat16)
    down_rows = w_down[0]
    result = jnp.dot(
        lax.all_gather(hidden, "seq", axis=1, tiled=True),
        down_rows,
        preferred_element_type=jnp.float32,
    )
    expert_out = result.astype(jnp.bfloat16)[None]
    returned = lax.all_to_all(expert_out, "exp", split_axis=1, concat_axis=0, tiled=True)
    picked = jnp.einsum(
        "aec,ecd->ad", assign_table, returned, preferred_element_type=jnp.float32
    ).reshape(block_rows, top_count, -1)
    weight = jnp.where(is_kept.reshape(block_rows, top_count), gate_probs, 0.0)
    expert_sum = jnp.sum(picked * weight[:, :, None], axis=1)
    return ((after_attn + expert_sum).astype(jnp.bfloat16), final_rows)


def solution(mesh):
    in_specs = (
        P("exp", "seq"),
        P("seq", "exp"),
        P("seq", "exp"),
        P("seq", "exp"),
        P("seq", "exp"),
        P("seq", "exp"),
        P("exp", None, None),
        P("exp"),
        P("exp", "seq"),
        P("seq"),
        P("seq", None),
        P("exp", "seq", None),
        P("exp", "seq", None),
        P("exp", None, "seq"),
        P("exp", None),
        P(),
    )
    out_specs = (P("exp", "seq"), P("exp", "seq", None))
    return jax.shard_map(local, mesh=mesh, in_specs=in_specs, out_specs=out_specs, check_vma=False)
```

profile of v0, /device:TPU:2, one launch (start us, length us, event | category | flops | bytes accessed | tf_op | source)
XLA Modules:
  0.0 770.6 jit_solution(17127196625241131130)
XLA Ops:
  7.2 1.6 copy.113
  8.8 1.6 reduce_window_sum.26
  11.1 1.5 subtract_exponential_fusion
  13.5 1.9 convert_multiply_fusion
  15.4 2.1 copy.145
  17.5 2.4 fusion.64
  21.5 42.1 %all-gather.2 = bf16[32,1,8]{2,1,0:T(2,128)(2,1)S(1)} all-gather(bf16[1,1,8]{2,1,0:T(2,128)(2,1)S(1)} %convert_bitcast_fusion), channel_id=1, replica_groups=mesh['seq'=32,'exp'=8] {'seq'}, dimensions={0}, use_global_device_ids=true | all-gather | bytes 528 | tf_op jit(solution)/shard_map/all_gather | solution.py:14
  63.6 1.5 copy.122
  65.2 2.0 convolution_multiply_fusion
  67.1 1.5 convolution_bitcast_fusion.1
  68.7 52.2 %all-gather.14.cloned.1.call-done = bf16[256,128,128]{2,1,0:T(8,128)(2,1)} async-done(((bf16[8,128,128]{2,1,0:T(8,128)(2,1)}), bf16[256,128,128]{2,1,0:T(8,128)(2,1)}) %all-gather.14.cloned.1.call-update) | async-done | bytes 8388624 | tf_op jit(solution)/shard_map/all_gather | solution.py:14
  121.8 2.7 multiply_reduce_fusion.1
  125.6 2.0 copy.125
  127.6 2.0 multiply_convert_fusion.2
  129.6 157.0 %all-gather.8.cloned.1.call-done = bf16[4096,1024]{1,0:T(8,128)(2,1)} async-done(((bf16[128,1024]{1,0:T(8,128)(2,1)}), bf16[4096,1024]{1,0:T(8,128)(2,1)}) %all-gather.8.cloned.1.call-update) | async-done | bytes 8388624 | tf_op jit(solution)/shard_map/all_gather | solution.py:123
  286.6 7.5 convolution_convert_fusion
  299.2 1.3 dynamic-update-slice
  300.4 8.1 %all-reduce = s32[64]{0:T(128)S(1)} all-reduce(s32[64]{0:T(128)} %dynamic-update-slice), channel_id=3, replica_groups=mesh['seq'=32,'exp'=8] {'exp'}, use_global_device_ids=true, to_apply=%add | all-reduce | flops 64 | bytes 512
  309.9 5.1 reduce-window.6
  316.1 1.5 add_bitcast_fusion
  317.6 1.4 while.23
  319.0 1.5 select_reduce_fusion.1
  320.4 1.6 reduce_sum.80
  322.0 1.7 copy.130
  323.7 1.6 reduce_sum.82
  325.3 1.7 copy.131
  329.5 2.2 fusion.42
  331.7 8.9 %fusion.36 = f32[512,2]{1,0:T(8,128)} fusion(f32[512,32]{1,0:T(8,128)S(1)} %fusion.42, s32[512,2]{1,0:T(8,128)} %copy.126), kind=kLoop, calls=%fused_computation.42 | loop fusion | flops 97280 | bytes 73728
  341.6 1.1 multiply_reduce_fusion.2
  342.7 73.0 %all-reduce.1 = (f32[512]{0:T(512)}, f32[512,2]{0,1:T(2,128)}) all-reduce(f32[512]{0:T(512)S(1)} %multiply_reduce_fusion.2, f32[512,2]{0,1:T(2,128)S(1)} %copy.141), channel_id=1, replica_groups=mesh['seq'=32,'exp'=8] {'seq'}, use_global_device_ids=true, to_apply=%region_15.16 | all-reduce | flops 1536 | bytes 12288 | tf_op jit(solution)/shard_map/psum | solution.py:138
  418.8 1.4 convolution_convert_fusion.1
  420.1 11.7 %all_to_all.24 = bf16[8,40,192]{2,1,0:T(8,128)(2,1)} all-to-all(bf16[8,40,192]{2,1,0:T(8,128)(2,1)S(1)} %convolution_convert_fusion.1), channel_id=1, replica_groups=mesh['seq'=32,'exp'=8] {'exp'}, dimensions={0} | all-to-all | bytes 245760 | tf_op jit(solution)/shard_map/all_to_all | solution.py:168
  431.8 1.7 copy.132
  433.6 79.5 %all-gather.10.cloned.1.call-done = bf16[1,320,6144]{1,2,0:T(8,128)(2,1)} async-done(((bf16[1,320,192]{1,2,0:T(8,128)(2,1)}), bf16[1,320,6144]{1,2,0:T(8,128)(2,1)}) %all-gather.10.cloned.1.call-update) | async-done | bytes 3932176 | tf_op jit(solution)/shard_map/all_gather | solution.py:170
  513.1 4.5 fusion
  518.0 2.7 fusion.16
  521.4 2.3 fusion.45
  523.7 86.0 %all-gather.12.cloned.1.call-done = bf16[320,9216]{0,1:T(8,128)(2,1)} async-done(((bf16[320,288]{0,1:T(8,128)(2,1)}), bf16[320,9216]{0,1:T(8,128)(2,1)}) %all-gather.12.cloned.1.call-update) | async-done | bytes 5898256 | tf_op jit(solution)/shard_map/all_gather | solution.py:180
  609.7 6.8 fusion.24
  616.5 1.8 copy.133
  618.8 3.2 reduce.4
  622.0 1.8 reshape.242
  623.8 4.8 all-to-all-start.1
  628.6 127.4 %all-reduce.4.cloned.1.call-done = bf16[8,128,128]{2,1,0:T(8,128)(2,1)} async-done(((bf16[8,128,128]{2,1,0:T(8,128)(2,1)}), bf16[8,128,128]{2,1,0:T(8,128)(2,1)}) %all-reduce.4.cloned.1.call-update) | async-done | bytes 262160 | tf_op jit(solution)/shard_map/psum | solution.py:33
  756.0 1.3 dynamic-slice_convert_fusion
  757.4 2.3 reshape.243
  760.6 1.4 fusion.9
  762.0 1.8 add_convert_fusion.1
  (72 shorter events, 22.9 us)
Async XLA Ops:
  7.2 506.0 %copy-start = (bf16[1,288,6144]{2,1,0:T(8,128)(2,1)S(1)}, bf16[1,288,6144]{2,1,0:T(8,128)(2,1)}, u32[]{:S(2)}) copy-start(bf16[1,288,6144]{2,1,0:T(8,128)(2,1)} %param.31) | copy-start | bytes 10616836
  7.2 113.7 %all-gather.14.cloned.1.call-start = ((), (), s32[]{:S(2)}) async-start(), calls=%async_computation.8 | async-start | bytes 8650752 | tf_op jit(solution)/shard_map/all_gather | solution.py:14
  19.9 266.7 %all-gather.8.cloned.1.call-start = ((), (), s32[]{:S(2)}) async-start(), calls=%async_computation.3 | async-start | bytes 8650752 | tf_op jit(solution)/shard_map/all_gather | solution.py:123
  65.1 2.0 copy-start.1
  121.7 2.8 copy-start.4
  121.8 3.8 copy-start.5
  129.6 164.6 %copy-start.3 = (s32[512,2]{0,1:T(2,128)S(1)}, s32[512,2]{0,1:T(2,128)}, u32[]{:S(2)}) copy-start(s32[512,2]{0,1:T(2,128)} %param.34) | copy-start | bytes 12292
  129.6 167.7 %copy-start.9 = (u32[256]{0:T(256)S(1)}, u32[256]{0:T(256)}, u32[]{:S(2)}) copy-start(u32[256]{0:T(256)} %constant.77) | copy-start | bytes 3076
  129.6 199.9 %reduce-scatter.2.cloned.1.call-start = ((), (), s32[]{:S(2)}) async-start(), calls=%async_computation.4 | async-start | bytes 1769472 | tf_op jit(solution)/shard_map/reduce_scatter | solution.py:125
  294.2 219.0 %all-gather.10.cloned.1.call-start = ((), (), s32[]{:S(2)}) async-start(), calls=%async_computation.5 | async-start | bytes 4866048 | tf_op jit(solution)/shard_map/all_gather | solution.py:170
  417.8 2.3 copy-start.2
  433.5 176.2 %all-gather.12.cloned.1.call-start = ((), (), s32[]{:S(2)}) async-start(), calls=%async_computation.6 | async-start | bytes 7299072 | tf_op jit(solution)/shard_map/all_gather | solution.py:180
  513.1 4.5 copy-start.7
  513.1 4.9 copy-start.8
  518.0 3.4 copy-start.6
  520.7 235.3 %all-reduce.4.cloned.1.call-start = ((), (), s32[]{:S(2)}) async-start(), calls=%async_computation.7 | async-start | bytes 524288 | tf_op jit(solution)/shard_map/psum | solution.py:33
  623.8 133.5 %all-to-all-start.1 = ((bf16[8,2,3840]{2,1,0:T(2,128)(2,1)}), bf16[8,2,3840]{2,1,0:T(2,128)(2,1)}, u32[]{:S(2)}, u32[]{:S(2)}) async-start(bf16[8,2,3840]{2,1,0:T(2,128)(2,1)} %reshape.242), calls=%async_computation.2 | async-start | bytes 245760 | tf_op jit(solution)/shard_map/all_to_all | solution.py:185
Sparse Core Ops, SparseCore 0:
  20.0 100.8 all-gather.13
  129.7 156.8 all-gather.7
  294.3 29.5 reduce-scatter.1
  433.7 79.4 all-gather.9
  520.8 88.8 all-gather.11
  613.0 142.9 all-reduce.3
where the time goes:
time: 774 us; the launch traced here: 771 us
  waiting for transfers between devices  502 us (65%)
  blocking collectives  135 us (17%)
  other arithmetic  40.5 us (5%)
  local copies, waits for them, and re-layouts  38 us (5%)
  matrix products  34.9 us (5%)
  between operations  15 us (2%)
    all_gather x1, waiting for transfers between devices, local(): gathered = lax.all_gather(heads_mixed, 'seq', axis=0, tiled=True)  157 us
    psum x1, waiting for transfers between devices, broadcast(): return lax.psum(kept, axis)  127 us
    all_gather x1, waiting for transfers between devices, local(): lax.all_gather(hidden, 'seq', axis=1, tiled=True)  86 us
    all_gather x1, waiting for transfers between devices, local(): portion = lax.all_gather(arrived, 'seq', axis=2, tiled=True)  79.5 us
    psum x1, blocking collectives, local(): lax.psum((jnp.sum(after_attn * after_attn, axis=1), chosen_part), 'seq')  73 us
    all_gather x1, waiting for transfers between devices, entering(): lax.all_gather(a.astype(kind), axis)  52.2 us
    all_gather x1, blocking collectives, entering(): lax.all_gather(a.astype(kind), axis)  42.1 us
  transfers between devices with their start and end apart: 7, of which 5 were waited for; matrix products, arithmetic and copies ran while one was open for 7% of the time, Pallas kernels for 0%

commit v1 on v0

--- a/solution.py
+++ b/solution.py
@@ -30,7 +30,7 @@
 
 def broadcast(value, axis, source):
     kept = jnp.where(lax.axis_index(axis) == source, value, 0).astype(value.dtype)
-    return lax.psum(kept, axis)
+    return jnp.sum(lax.all_gather(kept, axis), axis=0)
 
 
 def entering_2(part, axis, combine, identity):

time: 774 us -> 742 us (0.959)
  waiting for transfers between devices: 502 us -> 463 us
    psum x1 -> x0, waiting for transfers between devices: 127 us -> none  [broadcast(): return lax.psum(kept, axis)]
    all_gather x0 -> x1, waiting for transfers between devices: none -> 89.9 us  [broadcast(): return jnp.sum(lax.all_gather(kept, axis), axis=0)]
  transfers between devices with their start and end apart: 7 -> 7, of which waited for: 5 -> 6; matrix products, arithmetic and copies ran while one was open for 7% -> 7% of each run, Pallas kernels for 0% -> 0%
where the time goes in v1:
time: 742 us; the launch traced here: 737 us
  waiting for transfers between devices  463 us (62%)
  blocking collectives  135 us (18%)
  other arithmetic  46.8 us (6%)
  local copies, waits for them, and re-layouts  38 us (5%)
  matrix products  34.9 us (5%)
  between operations  15 us (2%)
    all_gather x1, waiting for transfers between devices, local(): gathered = lax.all_gather(heads_mixed, 'seq', axis=0, tiled=True)  156 us
    all_gather x1, waiting for transfers between devices, broadcast(): return jnp.sum(lax.all_gather(kept, axis), axis=0)  89.9 us
    all_gather x1, waiting for transfers between devices, local(): lax.all_gather(hidden, 'seq', axis=1, tiled=True)  85 us
    all_gather x1, waiting for transfers between devices, local(): portion = lax.all_gather(arrived, 'seq', axis=2, tiled=True)  76.5 us
    psum x1, blocking collectives, local(): lax.psum((jnp.sum(after_attn * after_attn, axis=1), chosen_part), 'seq')  73 us
    all_gather x1, waiting for transfers between devices, entering(): lax.all_gather(a.astype(kind), axis)  52.2 us
    all_gather x1, blocking collectives, entering(): lax.all_gather(a.astype(kind), axis)  42.1 us
  transfers between devices with their start and end apart: 7, of which 6 were waited for; matrix products, arithmetic and copies ran while one was open for 7% of the time, Pallas kernels for 0%

profile of v1, /device:TPU:2, one launch (start us, length us, event | category | flops | bytes accessed | tf_op | source)
XLA Modules:
  0.0 737.4 jit_solution(5302723025053218818)
XLA Ops:
  7.2 1.6 copy.113
  8.8 1.6 reduce_window_sum.26
  11.1 1.5 subtract_exponential_fusion
  13.5 1.9 convert_multiply_fusion
  15.4 2.1 copy.145
  17.4 2.4 fusion.64
  21.5 42.1 %all-gather.3 = bf16[32,1,8]{2,1,0:T(2,128)(2,1)S(1)} all-gather(bf16[1,1,8]{2,1,0:T(2,128)(2,1)S(1)} %convert_bitcast_fusion), channel_id=1, replica_groups=mesh['seq'=32,'exp'=8] {'seq'}, dimensions={0}, use_global_device_ids=true | all-gather | bytes 528 | tf_op jit(solution)/shard_map/all_gather | solution.py:14
  63.6 1.5 copy.122
  65.1 2.0 convolution_multiply_fusion
  67.1 1.6 convolution_bitcast_fusion.1
  68.7 52.2 %all-gather.16.cloned.1.call-done = bf16[256,128,128]{2,1,0:T(8,128)(2,1)} async-done(((bf16[8,128,128]{2,1,0:T(8,128)(2,1)}), bf16[256,128,128]{2,1,0:T(8,128)(2,1)}) %all-gather.16.cloned.1.call-update) | async-done | bytes 8388624 | tf_op jit(solution)/shard_map/all_gather | solution.py:14
  121.7 2.7 multiply_reduce_fusion.1
  125.5 2.0 copy.125
  127.5 2.0 multiply_convert_fusion.2
  129.6 155.6 %all-gather.10.cloned.1.call-done = bf16[4096,1024]{1,0:T(8,128)(2,1)} async-done(((bf16[128,1024]{1,0:T(8,128)(2,1)}), bf16[4096,1024]{1,0:T(8,128)(2,1)}) %all-gather.10.cloned.1.call-update) | async-done | bytes 8388624 | tf_op jit(solution)/shard_map/all_gather | solution.py:123
  285.2 7.5 %convolution_convert_fusion = bf16[4096,192]{0,1:T(8,128)(2,1)} fusion(bf16[4096,1024]{1,0:T(8,128)(2,1)} %all-gather.10.cloned.1.call-done, bf16[1024,192]{0,1:T(8,128)(2,1)} %param.28), kind=kOutput, calls=%fused_computation.5 | convolution fusion | flops 1611399168 | bytes 10354688 | tf_op jit(solution)/shard_map/dot_general | solution.py:126
  299.0 8.1 %all-reduce = s32[64]{0:T(128)S(1)} all-reduce(s32[64]{0:T(128)} %dynamic-update-slice), channel_id=3, replica_groups=mesh['seq'=32,'exp'=8] {'exp'}, use_global_device_ids=true, to_apply=%add | all-reduce | flops 64 | bytes 512
  308.5 5.1 reduce-window.6
  314.7 1.5 add_bitcast_fusion
  316.2 1.4 while.23
  317.6 1.5 select_reduce_fusion.1
  319.0 1.6 reduce_sum.92
  320.6 1.7 copy.130
  322.3 1.6 reduce_sum.94
  323.9 1.7 copy.131
  328.1 2.2 fusion.42
  330.3 8.9 %fusion.36 = f32[512,2]{1,0:T(8,128)} fusion(f32[512,32]{1,0:T(8,128)S(1)} %fusion.42, s32[512,2]{1,0:T(8,128)} %copy.126), kind=kLoop, calls=%fused_computation.42 | loop fusion | flops 97280 | bytes 73728
  341.4 73.0 %all-reduce.1 = (f32[512]{0:T(512)}, f32[512,2]{0,1:T(2,128)}) all-reduce(f32[512]{0:T(512)S(1)} %multiply_reduce_fusion.2, f32[512,2]{0,1:T(2,128)S(1)} %copy.141), channel_id=1, replica_groups=mesh['seq'=32,'exp'=8] {'seq'}, use_global_device_ids=true, to_apply=%region_15.16 | all-reduce | flops 1536 | bytes 12288 | tf_op jit(solution)/shard_map/psum | solution.py:138
  417.4 1.4 convolution_convert_fusion.1
  418.8 11.7 %all_to_all.24 = bf16[8,40,192]{2,1,0:T(8,128)(2,1)} all-to-all(bf16[8,40,192]{2,1,0:T(8,128)(2,1)S(1)} %convolution_convert_fusion.1), channel_id=1, replica_groups=mesh['seq'=32,'exp'=8] {'exp'}, dimensions={0} | all-to-all | bytes 245760 | tf_op jit(solution)/shard_map/all_to_all | solution.py:168
  430.5 1.7 copy.132
  432.9 2.2 fusion.45
  435.2 76.5 %all-gather.12.cloned.1.call-done = bf16[1,320,6144]{1,2,0:T(8,128)(2,1)} async-done(((bf16[1,320,192]{1,2,0:T(8,128)(2,1)}), bf16[1,320,6144]{1,2,0:T(8,128)(2,1)}) %all-gather.12.cloned.1.call-update) | async-done | bytes 3932176 | tf_op jit(solution)/shard_map/all_gather | solution.py:170
  511.8 4.5 fusion
  516.6 2.7 fusion.16
  519.3 89.9 %all-gather.18.cloned.1.call-done = bf16[256,128,128]{2,1,0:T(8,128)(2,1)} async-done(((bf16[8,128,128]{2,1,0:T(8,128)(2,1)}), bf16[256,128,128]{2,1,0:T(8,128)(2,1)}) %all-gather.18.cloned.1.call-update) | async-done | bytes 8388624 | tf_op jit(solution)/shard_map/all_gather | solution.py:33
  609.3 6.3 reduce_sum.98
  615.6 85.0 %all-gather.14.cloned.1.call-done = bf16[320,9216]{0,1:T(8,128)(2,1)} async-done(((bf16[320,288]{0,1:T(8,128)(2,1)}), bf16[320,9216]{0,1:T(8,128)(2,1)}) %all-gather.14.cloned.1.call-update) | async-done | bytes 5898256 | tf_op jit(solution)/shard_map/all_gather | solution.py:180
  700.6 6.8 fusion.24
  707.3 1.8 copy.133
  709.7 3.2 reduce.5
  712.9 1.8 reshape.243
  714.6 4.8 all-to-all-start.1
  719.5 1.3 dynamic-slice_convert_fusion
  720.8 3.3 all-to-all-done.1
  724.1 2.3 reshape.244
  727.4 1.4 fusion.9
  728.7 1.8 add_convert_fusion.1
  (71 shorter events, 25.2 us)
Async XLA Ops:
  7.2 504.6 %copy-start = (bf16[1,288,6144]{2,1,0:T(8,128)(2,1)S(1)}, bf16[1,288,6144]{2,1,0:T(8,128)(2,1)}, u32[]{:S(2)}) copy-start(bf16[1,288,6144]{2,1,0:T(8,128)(2,1)} %param.31) | copy-start | bytes 10616836
  7.2 113.7 %all-gather.16.cloned.1.call-start = ((), (), s32[]{:S(2)}) async-start(), calls=%async_computation.7 | async-start | bytes 8650752 | tf_op jit(solution)/shard_map/all_gather | solution.py:14
  19.9 265.3 %all-gather.10.cloned.1.call-start = ((), (), s32[]{:S(2)}) async-start(), calls=%async_computation.3 | async-start | bytes 8650752 | tf_op jit(solution)/shard_map/all_gather | solution.py:123
  65.1 2.0 copy-start.1
  121.7 2.8 copy-start.4
  121.7 3.8 copy-start.5
  129.5 163.3 %copy-start.3 = (s32[512,2]{0,1:T(2,128)S(1)}, s32[512,2]{0,1:T(2,128)}, u32[]{:S(2)}) copy-start(s32[512,2]{0,1:T(2,128)} %param.34) | copy-start | bytes 12292
  129.5 166.4 %copy-start.8 = (u32[256]{0:T(256)S(1)}, u32[256]{0:T(256)}, u32[]{:S(2)}) copy-start(u32[256]{0:T(256)} %constant.78) | copy-start | bytes 3076
  129.5 198.6 %reduce-scatter.2.cloned.1.call-start = ((), (), s32[]{:S(2)}) async-start(), calls=%async_computation.4 | async-start | bytes 1769472 | tf_op jit(solution)/shard_map/reduce_scatter | solution.py:125
  292.7 219.0 %all-gather.12.cloned.1.call-start = ((), (), s32[]{:S(2)}) async-start(), calls=%async_computation.5 | async-start | bytes 4866048 | tf_op jit(solution)/shard_map/all_gather | solution.py:170
  416.5 2.3 copy-start.2
  432.2 177.1 %all-gather.18.cloned.1.call-start = ((), (), s32[]{:S(2)}) async-start(), calls=%async_computation.8 | async-start | bytes 8650752 | tf_op jit(solution)/shard_map/all_gather | solution.py:33
  435.2 265.4 %all-gather.14.cloned.1.call-start = ((), (), s32[]{:S(2)}) async-start(), calls=%async_computation.6 | async-start | bytes 7299072 | tf_op jit(solution)/shard_map/all_gather | solution.py:180
  511.8 4.5 copy-start.6
  511.8 4.9 copy-start.7
  714.6 9.5 %all-to-all-start.1 = ((bf16[8,2,3840]{2,1,0:T(2,128)(2,1)}), bf16[8,2,3840]{2,1,0:T(2,128)(2,1)}, u32[]{:S(2)}, u32[]{:S(2)}) async-start(bf16[8,2,3840]{2,1,0:T(2,128)(2,1)} %reshape.243), calls=%async_computation.2 | async-start | bytes 245760 | tf_op jit(solution)/shard_map/all_to_all | solution.py:185
Sparse Core Ops, SparseCore 0:
  20.0 100.8 all-gather.15
  129.6 155.5 all-gather.9
  292.9 29.4 reduce-scatter.1
  432.3 79.4 all-gather.11
  514.2 95.0 all-gather.17
  611.7 88.8 all-gather.13
